TPU v7x, 128 devices: a whole 4x4x4 slice. The times are simulated.
128 devices in a mesh: slot: 16 (over y, z), head: 2 (over x_lo), conv: 4 (over x_hi, core).
Axes of the slice: x: 4 (x_hi: 2, x_lo: 2; x = x_hi * 2 + x_lo), y: 4, z: 4, core: 2. Of those that a mesh axis runs over, the one named last changes fastest.
Arguments:
- queries: bfloat16 [1024, 64, 128], P(('conv', 'slot'), 'head'), may hold values from -96 to 96
- out_grad: bfloat16 [1024, 64, 128], P(('conv', 'slot'), 'head'), may hold values from -768 to 768
- row_positions: int32 [1024], P('conv'), may hold values from 0 to 8191
- slot_offsets: int32 [16384], P('slot'), may hold values from 0 to 16382, as said below
- cache: float32 [2, 16384, 4, 128], P(None, 'slot', 'head'), may hold values from -12 to 12
- first_moment: float32 [2, 16384, 4, 128], P(None, 'slot', 'head'), may hold values from -6 to 6
- second_moment: float32 [2, 16384, 4, 128], P(None, 'slot', 'head'), may hold values from 0.01 to 1000
Outputs:
- new_cache: float32 [2, 16384, 4, 128], P(None, 'slot', 'head')
- new_first_moment: float32 [2, 16384, 4, 128], P(None, 'slot', 'head')
- new_second_moment: float32 [2, 16384, 4, 128], P(None, 'slot', 'head')
- query_grad: float32 [1024, 64, 128], P(('conv', 'slot'), 'head')
Inputs may be any that keep to these rules, and one draw needn't show every extreme that they name: `slot_offsets`: never falls from one slot to the next; its first two entries are 0.
All inputs are finite; a program needn't handle non-finite values.
Results may differ from a plain program's by a relative error of at most 0.012.
The roundings to bfloat16 on the way count: a program that leaves them out, or rounds other values in their place, can miss the bound.
Values may be sent and summed in bfloat16 or wider, within the bound.
A program may use at most 128 MiB of HBM per device.

v0:
```python
import math
import jax
import jax.numpy as jnp
from jax import lax
from jax.sharding import PartitionSpec as P

STEP = 20
learn_rate = 0.01
beta_one = 0.9
beta_two = 0.95
adam_eps = 1e-08
masked_score = -1e30


def merged(x, axis, combine):
    everything = jax.tree.map(lambda part: lax.all_gather(part, axis), x)
    leading = jax.tree.map(lambda part: part[0], everything)

    def lap(k, so_far):
        return combine(so_far, jax.tree.map(lambda part: part[k], everything))

    return lax.fori_loop(1, lax.axis_size(axis), lap, leading)


def merge_pairs(earlier, later):
    largest = jnp.maximum(earlier[0], later[0])
    return (
        largest,
        earlier[1] * jnp.exp(earlier[0] - largest) + later[1] * jnp.exp(later[0] - largest),
    )


def local(queries, out_grad, row_positions, slot_offsets, cache, first_moment, second_moment):
    query_all, grad_all = (
        lax.all_gather(queries, "slot", axis=0, tiled=True),
        lax.all_gather(out_grad, "slot", axis=0, tiled=True),
    )
    total_rows, head_count, head_width = query_all.shape
    kv_count = cache.shape[2]
    group_heads = head_count // kv_count
    score_scale = 1.0 / math.sqrt(head_width)
    block_rows = min(64, total_rows)
    block_count = total_rows // block_rows
    key_half = cache[0].astype(jnp.bfloat16)
    value_half = cache[1].astype(jnp.bfloat16)
    query_blocks = query_all.reshape(block_count, block_rows, kv_count, group_heads, head_width)
    grad_blocks = grad_all.reshape(block_count, block_rows, kv_count, group_heads, head_width)
    visible_all = (slot_offsets[None, :] <= row_positions[:, None]).reshape(
        block_count, block_rows, -1
    )

    def masked_scores(query_block, visible):
        raw_score = (
            jnp.einsum("rkgd,skd->rkgs", query_block, key_half, preferred_element_type=jnp.float32)
            * score_scale
        )
        return jnp.where(visible[:, None, None, :], raw_score, masked_score)

    def weights_from(scores, visible, offset):
        return jnp.where(visible[:, None, None, :], jnp.exp(scores - offset[..., None]), 0.0)

    def gradient_products(grad_block):
        return jnp.einsum(
            "rkgd,skd->rkgs", grad_block, value_half, preferred_element_type=jnp.float32
        )

    def max_pass(inputs):
        query_block, visible = inputs
        scores = masked_scores(query_block, visible)
        largest = jnp.max(scores, axis=-1)
        return (largest, jnp.sum(weights_from(scores, visible, largest), axis=-1))

    largest, denominator = lax.map(max_pass, (query_blocks, visible_all))
    largest, denominator = merged((largest, denominator), "slot", merge_pairs)
    log_total = largest + jnp.log(denominator)

    def product_pass(inputs):
        query_block, grad_block, visible, block_total = inputs
        probability = weights_from(masked_scores(query_block, visible), visible, block_total)
        return jnp.sum(probability * gradient_products(grad_block), axis=-1)

    partial_sum = lax.map(product_pass, (query_blocks, grad_blocks, visible_all, log_total))
    row_sum = lax.psum(partial_sum, "slot")

    def last_pass(running, inputs):
        key_grad, value_grad = running
        query_block, grad_block, visible, block_total, block_sum = inputs
        probability = weights_from(masked_scores(query_block, visible), visible, block_total)
        prob_grad = gradient_products(grad_block)
        score_grad = (probability * (prob_grad - block_sum[..., None])).astype(jnp.bfloat16)
        prob_half = probability.astype(jnp.bfloat16)
        value_grad = value_grad + jnp.einsum(
            "rkgs,rkgd->skd", prob_half, grad_block, preferred_element_type=jnp.float32
        )
        key_grad = (
            key_grad
            + jnp.einsum(
                "rkgs,rkgd->skd", score_grad, query_block, preferred_element_type=jnp.float32
            )
            * score_scale
        )
        query_part = (
            jnp.einsum("rkgs,skd->rkgd", score_grad, key_half, preferred_element_type=jnp.float32)
            * score_scale
        )
        return ((key_grad, value_grad), query_part)

    empty_grad = jnp.zeros(key_half.shape, jnp.float32)
    (key_grad, value_grad), query_parts = lax.scan(
        last_pass,
        (empty_grad, empty_grad),
        (query_blocks, grad_blocks, visible_all, log_total, row_sum),
    )
    query_terms = query_parts.reshape(total_rows, head_count, head_width)
    summed = lax.psum(query_terms, "slot")
    own_rows = queries.shape[0]
    query_grad = lax.dynamic_slice_in_dim(summed, lax.axis_index("slot") * own_rows, own_rows, 0)
    key_total, value_total = lax.psum((key_grad, value_grad), "conv")
    slot_grad = jnp.stack([key_total, value_total])
    new_first = beta_one * first_moment + (1.0 - beta_one) * slot_grad
    new_second = beta_two * second_moment + (1.0 - beta_two) * slot_grad * slot_grad
    first_fix = 1.0 - beta_one**STEP
    second_fix = 1.0 - beta_two**STEP
    new_cache = cache - learn_rate * (new_first / first_fix) / (
        jnp.sqrt(new_second / second_fix) + adam_eps
    )
    return (new_cache, new_first, new_second, query_grad)


def solution(mesh):
    in_specs = (
        P(("conv", "slot"), "head", None),
        P(("conv", "slot"), "head", None),
        P("conv"),
        P("slot"),
        P(None, "slot", "head", None),
        P(None, "slot", "head", None),
        P(None, "slot", "head", None),
    )
    out_specs = (
        P(None, "slot", "head", None),
        P(None, "slot", "head", None),
        P(None, "slot", "head", None),
        P(("conv", "slot"), "head", None),
    )
    return jax.shard_map(local, mesh=mesh, in_specs=in_specs, out_specs=out_specs, check_vma=False)
```

profile of v0, /device:TPU:1, one launch (start us, length us, event | category | flops | bytes accessed | tf_op | source)
XLA Modules:
  0.0 525.3 jit_solution(10511550598650439508)
XLA Ops:
  9.5 1.8 copy.70
  13.1 43.8 %all-gather.5.cloned.1.call-done = bf16[256,32,128]{2,1,0:T(8,128)(2,1)} async-done(((bf16[16,32,128]{2,1,0:T(8,128)(2,1)}), bf16[256,32,128]{2,1,0:T(8,128)(2,1)}) %all-gather.5.cloned.1.call-update) | async-done | bytes 2097168 | tf_op jit(solution)/shard_map/all_gather | solution.py:35
  56.9 3.3 copy.50
  60.1 43.2 %all-gather.7.cloned.1.call-done = bf16[256,32,128]{2,1,0:T(8,128)(2,1)} async-done(((bf16[16,32,128]{2,1,0:T(8,128)(2,1)}), bf16[256,32,128]{2,1,0:T(8,128)(2,1)}) %all-gather.7.cloned.1.call-update) | async-done | bytes 2097168 | tf_op jit(solution)/shard_map/all_gather | solution.py:36
  103.3 3.3 copy.51
  106.6 23.2 %while.54 = (s32[]{:T(128)}, f32[4,64,2,16]{1,3,2,0:T(8,128)S(1)}, f32[4,64,2,16]{1,3,2,0:T(8,128)S(1)}, pred[4,64,1024]{2,1,0:T(8,128)(4,1)S(1)}, bf16[4,64,2,1...) while((s32[]{:T(128)}, f32[4,64,2,16]{1,3,2,0:T(8,128)S(1)}, ...), condition=%wide.region_3.4_spmd, body=%wide.region_0.3_spmd.sunk | while | flops 553644032 | bytes 18210912 | solution.py:73
  106.6 2.8 bitcast_reduce_fusion.2
  109.4 2.8 fusion.87
  112.4 2.8 bitcast_reduce_fusion.2
  115.2 2.8 fusion.87
  118.2 2.8 bitcast_reduce_fusion.2
  121.0 2.8 fusion.87
  124.0 2.8 bitcast_reduce_fusion.2
  126.8 2.8 fusion.87
  129.8 19.1 %all-gather.1 = f32[64,64,2,16]{1,3,2,0:T(8,128)S(1)} all-gather(f32[4,64,2,16]{1,3,2,0:T(8,128)S(1)} %get-tuple-element.272), channel_id=3, replica_groups=mesh['slot'=16,'head'=2,'conv'=4] {'slot'}, dimensions={0}, use_global_device_ids=true | all-gather | bytes 557056 | tf_op jit(solution)/shard_map/all_gather | solution.py:16
  148.9 17.4 %all-gather = f32[64,64,2,16]{1,3,2,0:T(8,128)S(1)} all-gather(f32[4,64,2,16]{1,3,2,0:T(8,128)S(1)} %get-tuple-element.271), channel_id=2, replica_groups=mesh['slot'=16,'head'=2,'conv'=4] {'slot'}, dimensions={0}, use_global_device_ids=true | all-gather | bytes 557056 | tf_op jit(solution)/shard_map/all_gather | solution.py:16
  167.2 13.9 %while.55 = (s32[]{:T(128)}, f32[4,64,2,16]{1,3,2,0:T(8,128)S(1)}, f32[4,64,2,16]{1,3,2,0:T(8,128)S(1)}, f32[16,4,64,2,16]{2,4,3,1,0:T(8,128)}, f32[16,4,64,2,16...) while((s32[]{:T(128)}, f32[4,64,2,16]{1,3,2,0:T(8,128)S(1)}, f32[4,64,2,16]{1,3,2,0:T(8,128)S(1)}, ...), condition=%wide.region_5.6_spmd, body=%wide.region_4.5_spmd.sunk | while | flops 49157 | bytes 196731 | solution.py:22
  181.5 31.2 %while.56 = (s32[]{:T(128)}, f32[4,64,2,16]{3,1,2,0:T(8,128)}, pred[4,64,1024]{2,1,0:T(8,128)(4,1)S(1)}, bf16[4,64,2,16,128]{4,3,1,2,0:T(8,128)(2,1)}, bf16[1024...) while((s32[]{:T(128)}, f32[4,64,2,16]{3,1,2,0:T(8,128)}, ...), condition=%wide.region_8.9_spmd, body=%wide.region_6.8_spmd.sunk | while | flops 1086322688 | bytes 21397652 | solution.py:82
  181.5 2.4 fusion.93
  183.9 4.7 fusion.94
  189.4 2.4 fusion.93
  191.7 4.7 fusion.94
  197.1 2.4 fusion.93
  199.5 4.7 fusion.94
  204.9 2.4 fusion.93
  207.3 4.7 fusion.94
  212.7 61.1 %psum.28 = f32[4,64,2,16]{3,1,2,0:T(8,128)S(1)} all-reduce(f32[4,64,2,16]{3,1,2,0:T(8,128)} %get-tuple-element.275), channel_id=1, replica_groups=mesh['slot'=16,'head'=2,'conv'=4] {'slot'}, use_global_device_ids=true, to_apply=%region_9.10 | all-reduce | flops 8192 | bytes 65536 | tf_op jit(solution)/shard_map/psum | solution.py:83
  273.8 52.7 %while.57 = (s32[]{:T(128)}, f32[1024,2,128]{0,2,1:T(8,128)S(1)}, f32[1024,2,128]{0,2,1:T(8,128)S(1)}, f32[4,64,2,16,128]{4,3,2,1,0:T(8,128)}, bf16[4,64,2,16,12...) while((s32[]{:T(128)}, f32[1024,2,128]{0,2,1:T(8,128)S(1)}, ...), condition=%wide.region_11.12_spmd.clone, body=%wide.region_10.11_spmd.clone.sunk | while | flops 2711093248 | bytes 59867360 | solution.py:109
  273.9 2.4 fusion.105
  276.4 2.7 fusion.108
  279.1 3.5 fusion.106
  282.5 2.1 fusion.107
  287.1 2.4 fusion.105
  289.6 2.7 fusion.108
  292.2 3.5 fusion.106
  295.7 2.1 fusion.107
  300.3 2.4 fusion.105
  302.7 2.7 fusion.108
  305.4 3.5 fusion.106
  308.9 2.1 fusion.107
  313.4 2.4 fusion.105
  315.9 2.7 fusion.108
  318.6 3.5 fusion.106
  322.1 2.1 fusion.107
  329.7 81.8 %all-reduce.6.cloned.1.call-done = (f32[1,1024,2,128]{3,2,1,0:T(2,128)}, f32[1,1024,2,128]{3,2,1,0:T(2,128)}) async-done(((f32[1,1024,2,128]{3,2,1,0:T(2,128)}, f32[1,1024,2,128]{3,2,1,0:T(2,128)}), (f32[1,1024,2,128]{3,2,1,0:T(2,128)}, f32[1,1024,2,128]{3,2,1,0:T(2,128)})) %all-reduce.6.cloned.1.call-update) | async-done | bytes 2097168 | tf_op jit(solution)/shard_map/psum | solution.py:118
  414.5 8.0 %divide_subtract_fusion = (f32[2,1024,2,128]{3,2,1,0:T(2,128)}, f32[2,1024,2,128]{3,2,1,0:T(2,128)}, f32[2,1024,2,128]{3,2,1,0:T(2,128)}) fusion(f32[2,1024,2,128]{3,2,1,0:T(2,128)S(1)} %copy-done, f32[2,1024,2,128]{3,2,1,0:T(2,128)S(1)} %constant_dynamic-update-slice_fusion.2, f32[2,1024,2,128]{3,2,1,0:T(2,128)S(1)} %copy-done.1, ...), kind=kLoop, calls=%fused_computation.80 | loop fusion | flops 6291456 | bytes 14680064 | tf_op jit(solution)/shard_map/sub | solution.py:124
  422.5 94.6 %all-reduce.4.cloned.1.call-done = f32[256,32,128]{2,1,0:T(8,128)} async-done(((f32[256,32,128]{2,1,0:T(8,128)}), f32[256,32,128]{2,1,0:T(8,128)}) %all-reduce.4.cloned.1.call-update) | async-done | bytes 4194320 | tf_op jit(solution)/shard_map/psum | solution.py:115
  517.1 1.7 constant_dynamic-slice_fusion
  (119 shorter events, 38.0 us)
Async XLA Ops:
  7.2 49.7 %all-gather.5.cloned.1.call-start = ((), (), s32[]{:S(2)}) async-start(), calls=%async_computation | async-start | bytes 2228224 | tf_op jit(solution)/shard_map/all_gather | solution.py:35
  7.9 95.4 %all-gather.7.cloned.1.call-start = ((), (), s32[]{:S(2)}) async-start(), calls=%async_computation.1 | async-start | bytes 2228224 | tf_op jit(solution)/shard_map/all_gather | solution.py:36
  8.6 402.9 %all-reduce.6.cloned.1.call-start = ((), (), s32[]{:S(2)}) async-start(), calls=%async_computation.3 | async-start | bytes 4194304 | tf_op jit(solution)/shard_map/psum | solution.py:118
  166.2 1.0 copy-start.4
  181.4 92.4 %copy-start.5 = (f32[1024,2,128]{0,2,1:T(8,128)S(1)}, f32[1024,2,128]{0,2,1:T(8,128)}, u32[]{:S(2)}) copy-start(f32[1024,2,128]{0,2,1:T(8,128)} %custom-call.1) | copy-start | bytes 3145732
  181.5 2.4 copy-start.6
  189.3 2.4 copy-start.6
  197.1 2.4 copy-start.6
  204.9 2.4 copy-start.6
  273.9 2.5 copy-start.3
  276.4 2.7 copy-start.7
  287.1 2.5 copy-start.3
  289.5 2.7 copy-start.7
  300.3 2.5 copy-start.3
  302.7 2.7 copy-start.7
  313.4 2.5 copy-start.3
  315.9 2.7 copy-start.7
  329.2 187.9 %all-reduce.4.cloned.1.call-start = ((), (), s32[]{:S(2)}) async-start(), calls=%async_computation.2 | async-start | bytes 8388608 | tf_op jit(solution)/shard_map/psum | solution.py:115
  329.2 85.2 %copy-start = (f32[2,1024,2,128]{3,2,1,0:T(2,128)S(1)}, f32[2,1024,2,128]{3,2,1,0:T(2,128)}, u32[]{:S(2)}) copy-start(f32[2,1024,2,128]{3,2,1,0:T(2,128)} %param.19) | copy-start | bytes 6291460
  411.5 3.0 copy-start.1
  411.5 3.0 copy-start.2
Sparse Core Ops, SparseCore 0:
  10.1 46.6 all-gather.4
  59.0 44.2 all-gather.6
  329.3 82.1 all-reduce.5
  414.7 102.2 all-reduce.3
where the time goes:
time: 527 us; the launch traced here: 525 us
  waiting for transfers between devices  265 us (50%)
  blocking collectives  97.6 us (19%)
  matrix products  87.3 us (17%)
  other arithmetic  33.9 us (6%)
  local copies, waits for them, and re-layouts  26.4 us (5%)
  between operations  13.9 us (3%)
    psum x1, waiting for transfers between devices, local(): summed = lax.psum(query_terms, 'slot')  94.6 us
    psum x1, waiting for transfers between devices, local(): key_total, value_total = lax.psum((key_grad, value_grad), 'conv')  81.8 us
    psum x1, blocking collectives, local(): row_sum = lax.psum(partial_sum, 'slot')  61.1 us
    all_gather x1, waiting for transfers between devices, local(): lax.all_gather(queries, 'slot', axis=0, tiled=True)  43.8 us
    all_gather x1, waiting for transfers between devices, local(): lax.all_gather(out_grad, 'slot', axis=0, tiled=True)  43.2 us
    all_gather x2, blocking collectives, merged(): everything = jax.tree.map(lambda part: lax.all_gather(part, axis), x)  36.5 us
    dot_general x8, matrix products, gradient_products(): jnp.einsum('rkgd,skd->rkgs', grad_block, value_half, preferred_element_ty...  32.8 us
    dot_general x12, matrix products, masked_scores(): jnp.einsum('rkgd,skd->rkgs', query_block, key_half, preferred_element_typ...  30.3 us
  transfers between devices with their start and end apart: 4, of which 4 were waited for; matrix products, arithmetic and copies ran while one was open for 4% of the time, Pallas kernels for 0%

commit v1 on v0

--- a/solution.py
+++ b/solution.py
@@ -33,7 +33,9 @@
 def local(queries, out_grad, row_positions, slot_offsets, cache, first_moment, second_moment):
     query_all, grad_all = (
         lax.all_gather(queries, "slot", axis=0, tiled=True),
-        lax.all_gather(out_grad, "slot", axis=0, tiled=True),
+        jnp.concatenate(
+            lax.all_to_all(jnp.stack([out_grad] * lax.axis_size("slot")), "slot", 0, 0), axis=0
+        ),
     )
     total_rows, head_count, head_width = query_all.shape
     kv_count = cache.shape[2]

time: 527 us -> 496 us (0.941)
  waiting for transfers between devices: 265 us -> 222 us
  starting transfers between devices: 0.16 us -> 8.89 us
    all_gather x1 -> x0, waiting for transfers between devices: 43.2 us -> none  [local(): lax.all_gather(out_grad, 'slot', axis=0, tiled=True)]
    all_to_all x0 -> x1, waiting for transfers between devices: none -> 27.2 us  [local(): lax.all_to_all(jnp.stack([out_grad] * lax.axis_size('slot')), 'slot', 0, 0)]
    all_gather x1, waiting for transfers between devices: 43.8 us -> 18.6 us  [local(): lax.all_gather(queries, 'slot', axis=0, tiled=True)]
    all_to_all x0 -> x1, starting transfers between devices: none -> 8.77 us  [local(): lax.all_to_all(jnp.stack([out_grad] * lax.axis_size('slot')), 'slot', 0, 0)]
    unnamed x14 -> x12, local copies, waits for them, and re-layouts: 10.8 us -> 10.6 us
where the time goes in v1:
time: 496 us; the launch traced here: 494 us
  waiting for transfers between devices  222 us (45%)
  blocking collectives  97.6 us (20%)
  matrix products  87.3 us (18%)
  other arithmetic  35.1 us (7%)
  local copies, waits for them, and re-layouts  28.1 us (6%)
  between operations  13.9 us (3%)
  starting transfers between devices  8.89 us (2%)
    psum x1, waiting for transfers between devices, local(): summed = lax.psum(query_terms, 'slot')  93.3 us
    psum x1, waiting for transfers between devices, local(): key_total, value_total = lax.psum((key_grad, value_grad), 'conv')  81.6 us
    psum x1, blocking collectives, local(): row_sum = lax.psum(partial_sum, 'slot')  61.1 us
    all_gather x2, blocking collectives, merged(): everything = jax.tree.map(lambda part: lax.all_gather(part, axis), x)  36.5 us
    dot_general x8, matrix products, gradient_products(): jnp.einsum('rkgd,skd->rkgs', grad_block, value_half, preferred_element_ty...  32.8 us
    dot_general x12, matrix products, masked_scores(): jnp.einsum('rkgd,skd->rkgs', query_block, key_half, preferred_element_typ...  30.3 us
    all_to_all x1, waiting for transfers between devices, local(): lax.all_to_all(jnp.stack([out_grad] * lax.axis_size('slot')), 'slot', 0, 0)  27.2 us
    all_gather x1, waiting for transfers between devices, local(): lax.all_gather(queries, 'slot', axis=0, tiled=True)  18.6 us
  transfers between devices with their start and end apart: 4, of which 4 were waited for; matrix products, arithmetic and copies ran while one was open for 4% of the time, Pallas kernels for 0%

profile of v1, /device:TPU:1, one launch (start us, length us, event | category | flops | bytes accessed | tf_op | source)
XLA Modules:
  0.0 493.7 jit_solution(15138083959505312015)
XLA Ops:
  7.9 2.6 stack.8
  10.5 8.8 %all-to-all-start = ((bf16[16,16,32,128]{3,2,1,0:T(8,128)(2,1)}), bf16[16,16,32,128]{3,2,1,0:T(8,128)(2,1)}, u32[]{:S(2)}, u32[]{:S(2)}) async-start(bf16[16,16,32,128]{3,2,1,0:T(8,128)(2,1)} %stack.8), calls=%async_computation | async-start | bytes 4194304 | tf_op jit(solution)/shard_map/all_to_all | solution.py:37
  22.4 27.2 %all-to-all-done = bf16[16,16,32,128]{3,2,1,0:T(8,128)(2,1)} async-done(((bf16[16,16,32,128]{3,2,1,0:T(8,128)(2,1)}), bf16[16,16,32,128]{3,2,1,0:T(8,128)(2,1)}, u32[]{:S(2)}, u32[]{:S(2)}) %all-to-all-start) | async-done | bytes 2097184 | tf_op jit(solution)/shard_map/all_to_all | solution.py:37
  49.7 3.3 copy.51
  53.0 18.6 %all-gather.4.cloned.1.call-done = bf16[256,32,128]{2,1,0:T(8,128)(2,1)} async-done(((bf16[16,32,128]{2,1,0:T(8,128)(2,1)}), bf16[256,32,128]{2,1,0:T(8,128)(2,1)}) %all-gather.4.cloned.1.call-update) | async-done | bytes 2097168 | tf_op jit(solution)/shard_map/all_gather | solution.py:35
  71.5 3.3 copy.50
  74.8 23.2 %while.54 = (s32[]{:T(128)}, f32[4,64,2,16]{1,3,2,0:T(8,128)S(1)}, f32[4,64,2,16]{1,3,2,0:T(8,128)S(1)}, pred[4,64,1024]{2,1,0:T(8,128)(4,1)S(1)}, bf16[4,64,2,1...) while((s32[]{:T(128)}, f32[4,64,2,16]{1,3,2,0:T(8,128)S(1)}, ...), condition=%wide.region_3.4_spmd, body=%wide.region_0.3_spmd.sunk | while | flops 553644032 | bytes 18210912 | solution.py:75
  74.8 2.8 bitcast_reduce_fusion.2
  77.6 2.8 fusion.87
  80.6 2.8 bitcast_reduce_fusion.2
  83.4 2.8 fusion.87
  86.4 2.8 bitcast_reduce_fusion.2
  89.2 2.8 fusion.87
  92.2 2.8 bitcast_reduce_fusion.2
  95.0 2.8 fusion.87
  98.0 19.1 %all-gather.1 = f32[64,64,2,16]{1,3,2,0:T(8,128)S(1)} all-gather(f32[4,64,2,16]{1,3,2,0:T(8,128)S(1)} %get-tuple-element.272), channel_id=3, replica_groups=mesh['slot'=16,'head'=2,'conv'=4] {'slot'}, dimensions={0}, use_global_device_ids=true | all-gather | bytes 557056 | tf_op jit(solution)/shard_map/all_gather | solution.py:16
  117.1 17.4 %all-gather = f32[64,64,2,16]{1,3,2,0:T(8,128)S(1)} all-gather(f32[4,64,2,16]{1,3,2,0:T(8,128)S(1)} %get-tuple-element.271), channel_id=2, replica_groups=mesh['slot'=16,'head'=2,'conv'=4] {'slot'}, dimensions={0}, use_global_device_ids=true | all-gather | bytes 557056 | tf_op jit(solution)/shard_map/all_gather | solution.py:16
  135.4 13.9 %while.55 = (s32[]{:T(128)}, f32[4,64,2,16]{1,3,2,0:T(8,128)S(1)}, f32[4,64,2,16]{1,3,2,0:T(8,128)S(1)}, f32[16,4,64,2,16]{2,4,3,1,0:T(8,128)}, f32[16,4,64,2,16...) while((s32[]{:T(128)}, f32[4,64,2,16]{1,3,2,0:T(8,128)S(1)}, f32[4,64,2,16]{1,3,2,0:T(8,128)S(1)}, ...), condition=%wide.region_5.6_spmd, body=%wide.region_4.5_spmd.sunk | while | flops 49157 | bytes 196731 | solution.py:22
  149.7 31.2 %while.56 = (s32[]{:T(128)}, f32[4,64,2,16]{3,1,2,0:T(8,128)}, pred[4,64,1024]{2,1,0:T(8,128)(4,1)S(1)}, bf16[4,64,2,16,128]{4,3,1,2,0:T(8,128)(2,1)}, bf16[1024...) while((s32[]{:T(128)}, f32[4,64,2,16]{3,1,2,0:T(8,128)}, ...), condition=%wide.region_8.9_spmd, body=%wide.region_6.8_spmd.sunk | while | flops 1086322688 | bytes 21397652 | solution.py:84
  149.7 2.4 fusion.93
  152.2 4.7 fusion.94
  157.6 2.4 fusion.93
  159.9 4.7 fusion.94
  165.4 2.4 fusion.93
  167.7 4.7 fusion.94
  173.1 2.4 fusion.93
  175.5 4.7 fusion.94
  180.9 61.1 %psum.28 = f32[4,64,2,16]{3,1,2,0:T(8,128)S(1)} all-reduce(f32[4,64,2,16]{3,1,2,0:T(8,128)} %get-tuple-element.275), channel_id=1, replica_groups=mesh['slot'=16,'head'=2,'conv'=4] {'slot'}, use_global_device_ids=true, to_apply=%region_9.10 | all-reduce | flops 8192 | bytes 65536 | tf_op jit(solution)/shard_map/psum | solution.py:85
  242.1 52.8 %while.57 = (s32[]{:T(128)}, f32[1024,2,128]{0,2,1:T(8,128)S(1)}, f32[1024,2,128]{0,2,1:T(8,128)S(1)}, f32[4,64,2,16,128]{4,3,2,1,0:T(8,128)}, bf16[4,64,2,16,12...) while((s32[]{:T(128)}, f32[1024,2,128]{0,2,1:T(8,128)S(1)}, ...), condition=%wide.region_11.12_spmd.clone, body=%wide.region_10.11_spmd.clone.sunk | while | flops 2711093248 | bytes 59867360 | solution.py:111
  242.1 2.4 fusion.105
  244.6 2.7 fusion.108
  247.3 3.5 fusion.106
  250.8 2.1 fusion.107
  255.3 2.4 fusion.105
  257.8 2.7 fusion.108
  260.5 3.5 fusion.106
  263.9 2.1 fusion.107
  268.5 2.4 fusion.105
  271.0 2.7 fusion.108
  273.7 3.5 fusion.106
  277.1 2.1 fusion.107
  281.6 2.4 fusion.105
  284.1 2.7 fusion.108
  286.8 3.5 fusion.106
  290.3 2.1 fusion.107
  298.1 81.6 %all-reduce.6.cloned.1.call-done = (f32[1,1024,2,128]{3,2,1,0:T(2,128)}, f32[1,1024,2,128]{3,2,1,0:T(2,128)}) async-done(((f32[1,1024,2,128]{3,2,1,0:T(2,128)}, f32[1,1024,2,128]{3,2,1,0:T(2,128)}), (f32[1,1024,2,128]{3,2,1,0:T(2,128)}, f32[1,1024,2,128]{3,2,1,0:T(2,128)})) %all-reduce.6.cloned.1.call-update) | async-done | bytes 2097168 | tf_op jit(solution)/shard_map/psum | solution.py:120
  382.4 9.8 %divide_subtract_fusion = (f32[2,1024,2,128]{3,2,1,0:T(2,128)}, f32[2,1024,2,128]{3,2,1,0:T(2,128)}, f32[2,1024,2,128]{3,2,1,0:T(2,128)}) fusion(f32[2,1024,2,128]{3,2,1,0:T(2,128)} %param.19, f32[2,1024,2,128]{3,2,1,0:T(2,128)S(1)} %constant_dynamic-update-slice_fusion.2, f32[2,1024,2,128]{3,2,1,0:T(2,128)} %param.20, f32[2,1024,2,128]{3,2,1,0:T(2,128)} %param.21), kind=kLoop, calls=%fused_computation.80 | loop fusion | flops 6291456 | bytes 14680064 | tf_op jit(solution)/shard_map/sub | solution.py:126
  392.2 93.3 %all-reduce.4.cloned.1.call-done = f32[256,32,128]{2,1,0:T(8,128)} async-done(((f32[256,32,128]{2,1,0:T(8,128)}), f32[256,32,128]{2,1,0:T(8,128)}) %all-reduce.4.cloned.1.call-update) | async-done | bytes 4194320 | tf_op jit(solution)/shard_map/psum | solution.py:117
  (117 shorter events, 39.2 us)
Async XLA Ops:
  7.2 12.3 %copy-start.6 = (s32[256]{0:T(256)S(1)}, s32[256]{0:T(256)}, u32[]{:S(2)}) copy-start(s32[256]{0:T(256)} %param.17) | copy-start | bytes 3076
  7.2 64.4 %all-gather.4.cloned.1.call-start = ((), (), s32[]{:S(2)}) async-start(), calls=%async_computation.1 | async-start | bytes 2228224 | tf_op jit(solution)/shard_map/all_gather | solution.py:35
  10.5 10.8 %copy-start.5 = (s32[1024]{0:T(1024)S(1)}, s32[1024]{0:T(1024)}, u32[]{:S(2)}) copy-start(s32[1024]{0:T(1024)} %param.18) | copy-start | bytes 12292
  10.5 39.1 %all-to-all-start = ((bf16[16,16,32,128]{3,2,1,0:T(8,128)(2,1)}), bf16[16,16,32,128]{3,2,1,0:T(8,128)(2,1)}, u32[]{:S(2)}, u32[]{:S(2)}) async-start(bf16[16,16,32,128]{3,2,1,0:T(8,128)(2,1)} %stack.8), calls=%async_computation | async-start | bytes 4194304 | tf_op jit(solution)/shard_map/all_to_all | solution.py:37
  19.3 360.4 %all-reduce.6.cloned.1.call-start = ((), (), s32[]{:S(2)}) async-start(), calls=%async_computation.3 | async-start | bytes 4194304 | tf_op jit(solution)/shard_map/psum | solution.py:120
  134.5 1.0 copy-start.1
  149.7 92.4 %copy-start.2 = (f32[1024,2,128]{0,2,1:T(8,128)S(1)}, f32[1024,2,128]{0,2,1:T(8,128)}, u32[]{:S(2)}) copy-start(f32[1024,2,128]{0,2,1:T(8,128)} %custom-call.1) | copy-start | bytes 3145732
  149.7 2.4 copy-start.3
  157.6 2.4 copy-start.3
  165.4 2.4 copy-start.3
  173.1 2.4 copy-start.3
  242.1 2.5 copy-start
  244.6 2.7 copy-start.4
  255.3 2.5 copy-start
  257.8 2.7 copy-start.4
  268.5 2.5 copy-start
  270.9 2.7 copy-start.4
  281.6 2.5 copy-start
  284.1 2.7 copy-start.4
  297.4 188.1 %all-reduce.4.cloned.1.call-start = ((), (), s32[]{:S(2)}) async-start(), calls=%async_computation.2 | async-start | bytes 8388608 | tf_op jit(solution)/shard_map/psum | solution.py:117
Sparse Core Ops, SparseCore 0:
  10.1 61.3 all-gather.3
  297.5 82.1 all-reduce.5
  383.1 102.3 all-reduce.3
